TPU v7x, 32 devices: a whole 2x2x4 slice. The times are simulated.
32 devices in a mesh: expert: 8 (over z, x), tensor: 4 (over y, core).
Axes of the slice: x: 2, y: 2, z: 4, core: 2. Of those that a mesh axis runs over, the one named last changes fastest.
Arguments:
- tokens: bfloat16 [1024, 4096], P('expert', 'tensor'), may hold values from -6 to 6
- expert_ids: int32 [1024, 8], P('expert'), may hold values from 0 to 15, all different within a row; in each aligned block of 128 rows (0 to 127, 128 to 255, ...) at most 96 rows name the same one
- combine_weight: float32 [1024, 8], P('expert'), may hold values from 0.05 to 0.5
- gate_weight: bfloat16 [16, 4096, 1024], P('expert', 'tensor'), may hold values from -0.09375 to 0.09375
- up_weight: bfloat16 [16, 4096, 1024], P('expert', 'tensor'), may hold values from -0.09375 to 0.09375
- down_weight: bfloat16 [16, 1024, 4096], P('expert', None, 'tensor'), may hold values from -0.1875 to 0.1875
- out_cotangent: bfloat16 [1024, 4096], P('expert', 'tensor'), may hold values from -3 to 3
Outputs:
- mixed: bfloat16 [1024, 4096], P('expert', 'tensor')
- token_grad: bfloat16 [1024, 4096], P('expert', 'tensor')
- combine_grad: float32 [1024, 8], P('expert')
- gate_grad: bfloat16 [16, 4096, 1024], P('expert', 'tensor')
- up_grad: bfloat16 [16, 4096, 1024], P('expert', 'tensor')
- down_grad: bfloat16 [16, 1024, 4096], P('expert', None, 'tensor')
Inputs may be any that keep to these rules, and one draw needn't show every extreme that they name: `expert_ids`: each row names 8 different experts. Among the rows of one device no expert is named by more than 96 rows, a bound that some block reaches.
All inputs are finite; a program needn't handle non-finite values.
Results may differ from a plain program's by a relative error of at most 0.023.
Values may be sent and summed in bfloat16 or wider, within the bound.
A program may use at most 128 MiB of HBM per device.

v0:
```python
import jax
import jax.numpy as jnp
from jax import lax
from jax.sharding import PartitionSpec as P

F32, BF16 = (jnp.float32, jnp.bfloat16)


def dot(form, left, right):
    return jnp.einsum(form, left, right, preferred_element_type=F32)


def per_device(
    tokens, expert_ids, combine_weight, gate_weight, up_weight, down_weight, out_cotangent
):
    groups = lax.axis_size("expert")
    shards = lax.axis_size("tensor")
    local = gate_weight.shape[0]
    width = tokens.shape[1]
    hidden = gate_weight.shape[2]
    rows = tokens.shape[0]
    top = expert_ids.shape[1]
    experts = local * groups
    capacity = 3 * rows * top // (2 * experts)
    slots = groups * capacity
    total = local * slots
    own = total // shards
    mine = lax.axis_index("expert")
    named = expert_ids[:, :, None] == jnp.arange(experts, dtype=jnp.int32)
    dense_weight = jnp.sum(jnp.where(named, combine_weight[:, :, None], 0.0), axis=1)
    weights_all = lax.all_gather(dense_weight, "expert", axis=0)
    tokens_all = lax.all_gather(tokens, "expert", axis=0)
    cotangent_all = lax.all_gather(out_cotangent, "expert", axis=0)
    weight_tok = lax.dynamic_slice_in_dim(weights_all, mine * local, local, 2)
    weight_tok = weight_tok.transpose(2, 0, 1)
    served = weight_tok > 0.0
    earlier = (jnp.arange(rows)[:, None] < jnp.arange(rows)[None, :]).astype(BF16)
    position = dot("ebs,st->ebt", served.astype(BF16), earlier)
    at_slot = jnp.where(served, position, -1.0).astype(jnp.int32)
    chosen = at_slot[:, :, None, :] == jnp.arange(capacity, dtype=jnp.int32)[:, None]
    place = chosen.astype(BF16)
    weight_slot = jnp.sum(jnp.where(chosen, weight_tok[:, :, None, :], 0.0), axis=3)
    weight_slot = weight_slot.reshape(total, 1)
    weight_own = lax.dynamic_slice_in_dim(weight_slot, lax.axis_index("tensor") * own, own, 0)

    def dispatch(values):
        return [
            dot("bct,btd->bcd", place[e], values).astype(BF16).reshape(slots, width)
            for e in range(local)
        ]

    def scatter_rows(parts):
        return lax.psum_scatter(
            jnp.concatenate(parts, axis=0), "tensor", scatter_dimension=0, tiled=True
        ).astype(F32)

    def gather_rows(value):
        full = lax.all_gather(value.astype(BF16), "tensor", axis=0, tiled=True)
        return full.reshape(local, slots, hidden)

    def combine(parts):
        total_sum = sum(
            (
                dot("bct,bcd->btd", place[e], parts[e].reshape(groups, capacity, width))
                for e in range(local)
            )
        )
        return lax.psum_scatter(
            total_sum.astype(BF16), "expert", scatter_dimension=0, tiled=True
        ).reshape(rows, width)

    routed = dispatch(tokens_all)
    gate = scatter_rows(
        [dot("cd,dk->ck", routed[e], gate_weight[e]).astype(BF16) for e in range(local)]
    )
    up = scatter_rows(
        [dot("cd,dk->ck", routed[e], up_weight[e]).astype(BF16) for e in range(local)]
    )
    incoming = dispatch(cotangent_all)
    pulled = scatter_rows(
        [dot("cd,kd->ck", incoming[e], down_weight[e]).astype(BF16) for e in range(local)]
    )
    sigma = jax.nn.sigmoid(gate)
    silu = gate * sigma
    act = silu * up
    weighted_act = gather_rows(weight_own * act)
    weighted_pull = weight_own * pulled
    gate_diff = gather_rows(weighted_pull * up * sigma * (1.0 + gate * (1.0 - sigma)))
    up_diff = gather_rows(weighted_pull * silu)
    pair_own = jnp.sum(act * pulled, axis=1)
    pair_all = lax.all_gather(pair_own, "tensor", axis=0, tiled=True)
    pair_all = pair_all.reshape(local, groups, capacity)
    pair_tok = jnp.sum(jnp.where(chosen, pair_all[:, :, :, None], 0.0), axis=2)
    pair_tok = lax.all_to_all(
        pair_tok.transpose(1, 0, 2), "expert", split_axis=0, concat_axis=0, tiled=True
    ).reshape(experts, rows)
    combine_grad = jnp.sum(jnp.where(named, pair_tok.T[:, None, :], 0.0), axis=2)
    mixed = combine(
        [dot("ck,kd->cd", weighted_act[e], down_weight[e]).astype(BF16) for e in range(local)]
    )
    token_grad = combine(
        [
            (
                dot("ck,dk->cd", gate_diff[e], gate_weight[e])
                + dot("ck,dk->cd", up_diff[e], up_weight[e])
            ).astype(BF16)
            for e in range(local)
        ]
    )
    down_grad = jnp.stack(
        [dot("ck,cd->kd", weighted_act[e], incoming[e]).astype(BF16) for e in range(local)]
    )
    gate_grad = jnp.stack(
        [dot("cd,ck->dk", routed[e], gate_diff[e]).astype(BF16) for e in range(local)]
    )
    up_grad = jnp.stack(
        [dot("cd,ck->dk", routed[e], up_diff[e]).astype(BF16) for e in range(local)]
    )
    return (mixed, token_grad, combine_grad, gate_grad, up_grad, down_grad)


def solution(mesh):
    wide, narrow = (P("expert", "tensor"), P("expert", None))
    deep, flat = (P("expert", "tensor", None), P("expert", None, "tensor"))
    return jax.shard_map(
        per_device,
        mesh=mesh,
        in_specs=(wide, narrow, narrow, deep, deep, flat, wide),
        out_specs=(wide, wide, narrow, deep, deep, flat),
        check_vma=False,
    )
```

profile of v0, /device:TPU:0, one launch (start us, length us, event | category | flops | bytes accessed | tf_op | source)
XLA Modules:
  0.0 485.3 jit_solution(2494550937460764869)
XLA Ops:
  9.4 32.6 %all-gather = f32[1024,16]{0,1:T(8,128)S(1)} all-gather(f32[128,16]{0,1:T(8,128)S(1)} %select_reduce_fusion.3), channel_id=2, replica_groups=mesh['expert'=8,'tensor'=4] {'expert'}, dimensions={0}, use_global_device_ids=true | all-gather | bytes 73728 | tf_op jit(solution)/shard_map/all_gather | solution.py:31
  42.3 20.0 %all-gather.16.cloned.1.call-done = bf16[1024,1024]{1,0:T(8,128)(2,1)} async-done(((bf16[128,1024]{1,0:T(8,128)(2,1)}), bf16[1024,1024]{1,0:T(8,128)(2,1)}) %all-gather.16.cloned.1.call-update) | async-done | bytes 2097168 | tf_op jit(solution)/shard_map/all_gather | solution.py:32
  62.3 2.3 convolution_convert_fusion.2
  69.6 2.0 pad_maximum_fusion.4
  71.7 40.4 %all-gather.18.cloned.1.call-done = bf16[1024,1024]{1,0:T(8,128)(2,1)} async-done(((bf16[128,1024]{1,0:T(8,128)(2,1)}), bf16[1024,1024]{1,0:T(8,128)(2,1)}) %all-gather.18.cloned.1.call-update) | async-done | bytes 2097168 | tf_op jit(solution)/shard_map/all_gather | solution.py:33
  112.1 2.3 convolution_convert_fusion
  119.5 2.0 pad_maximum_fusion.5
  122.0 3.7 fusion.40
  127.5 2.0 pad_maximum_fusion.3
  129.6 22.1 %reduce-scatter.8.cloned.1.call-done = bf16[384,1024]{1,0:T(8,128)(2,1)} async-done(((bf16[1536,1024]{1,0:T(8,128)(2,1)}), bf16[384,1024]{1,0:T(8,128)(2,1)}) %reduce-scatter.8.cloned.1.call-update) | async-done | bytes 786448 | tf_op jit(solution)/shard_map/reduce_scatter | solution.py:53
  151.6 40.9 %reduce-scatter.12.cloned.1.call-done = bf16[384,1024]{1,0:T(8,128)(2,1)} async-done(((bf16[1536,1024]{1,0:T(8,128)(2,1)}), bf16[384,1024]{1,0:T(8,128)(2,1)}) %reduce-scatter.12.cloned.1.call-update) | async-done | bytes 786448 | tf_op jit(solution)/shard_map/reduce_scatter | solution.py:53
  192.5 40.9 %reduce-scatter.6.cloned.1.call-done = bf16[384,1024]{1,0:T(8,128)(2,1)} async-done(((bf16[1536,1024]{1,0:T(8,128)(2,1)}), bf16[384,1024]{1,0:T(8,128)(2,1)}) %reduce-scatter.6.cloned.1.call-update) | async-done | bytes 786448 | tf_op jit(solution)/shard_map/reduce_scatter | solution.py:53
  233.4 2.3 fusion.65
  235.7 5.2 %all-gather.3 = f32[4,1,384]{2,1,0:T(1,128)S(1)} all-gather(f32[1,1,384]{2,1,0:T(1,128)S(1)} %reshape.84), channel_id=1, replica_groups=mesh['expert'=8,'tensor'=4] {'tensor'}, dimensions={0}, use_global_device_ids=true | all-gather | bytes 7680 | tf_op jit(solution)/shard_map/all_gather | solution.py:91
  241.8 2.6 fusion.64
  245.9 27.1 %all-gather.10.cloned.1.call-done = bf16[1536,1024]{1,0:T(8,128)(2,1)} async-done(((bf16[384,1024]{1,0:T(8,128)(2,1)}), bf16[1536,1024]{1,0:T(8,128)(2,1)}) %all-gather.10.cloned.1.call-update) | async-done | bytes 3145744 | tf_op jit(solution)/shard_map/all_gather | solution.py:58
  273.0 4.0 fusion.49
  281.0 2.1 add_convert_fusion.1
  283.3 20.3 %all-gather.14.cloned.1.call-done = bf16[1536,1024]{1,0:T(8,128)(2,1)} async-done(((bf16[384,1024]{1,0:T(8,128)(2,1)}), bf16[1536,1024]{1,0:T(8,128)(2,1)}) %all-gather.14.cloned.1.call-update) | async-done | bytes 3145744 | tf_op jit(solution)/shard_map/all_gather | solution.py:58
  303.7 3.9 fusion.12
  307.6 26.8 %all-gather.12.cloned.1.call-done = bf16[1536,1024]{1,0:T(8,128)(2,1)} async-done(((bf16[384,1024]{1,0:T(8,128)(2,1)}), bf16[1536,1024]{1,0:T(8,128)(2,1)}) %all-gather.12.cloned.1.call-update) | async-done | bytes 3145744 | tf_op jit(solution)/shard_map/all_gather | solution.py:58
  334.3 4.1 add_convert_fusion.3
  345.6 2.2 add_convert_fusion
  347.9 12.2 %all_to_all.5 = f32[8,2,128]{2,1,0:T(2,128)S(1)} all-to-all(f32[8,2,128]{2,1,0:T(2,128)S(1)} %copy.26), channel_id=1, replica_groups=mesh['expert'=8,'tensor'=4] {'expert'}, dimensions={0} | all-to-all | bytes 16384 | tf_op jit(solution)/shard_map/all_to_all | solution.py:94
  360.7 3.4 convert_bitcast_fusion.4
  364.1 1.9 convert_bitcast_fusion.5
  366.0 2.5 pad_maximum_fusion
  371.2 1.9 convert_bitcast_fusion.3
  373.1 2.5 pad_maximum_fusion.1
  380.7 2.4 pad_maximum_fusion.2
  383.1 23.7 %reduce-scatter.10.cloned.1.call-done = bf16[1,128,1024]{2,1,0:T(8,128)(2,1)} async-done(((bf16[8,128,1024]{2,1,0:T(8,128)(2,1)}), bf16[1,128,1024]{2,1,0:T(8,128)(2,1)}) %reduce-scatter.10.cloned.1.call-update) | async-done | bytes 262160 | tf_op jit(solution)/shard_map/reduce_scatter | solution.py:68
  406.8 71.4 %reduce-scatter.14.cloned.1.call-done = bf16[1,128,1024]{2,1,0:T(8,128)(2,1)} async-done(((bf16[8,128,1024]{2,1,0:T(8,128)(2,1)}), bf16[1,128,1024]{2,1,0:T(8,128)(2,1)}) %reduce-scatter.14.cloned.1.call-update) | async-done | bytes 262160 | tf_op jit(solution)/shard_map/reduce_scatter | solution.py:68
  (100 shorter events, 37.2 us)
Async XLA Ops:
  7.2 55.1 %all-gather.16.cloned.1.call-start = ((), (), s32[]{:S(2)}) async-start(), calls=%async_computation.14 | async-start | bytes 2359296 | tf_op jit(solution)/shard_map/all_gather | solution.py:32
  7.9 104.2 %all-gather.18.cloned.1.call-start = ((), (), s32[]{:S(2)}) async-start(), calls=%async_computation.15 | async-start | bytes 2359296 | tf_op jit(solution)/shard_map/all_gather | solution.py:33
  8.6 143.0 %reduce-scatter.8.cloned.1.call-start = ((), (), s32[]{:S(2)}) async-start(), calls=%async_computation.7 | async-start | bytes 3932160 | tf_op jit(solution)/shard_map/reduce_scatter | solution.py:53
  62.3 2.3 copy-start.1
  62.3 3.8 copy-start.16
  64.6 57.4 %copy-start.7 = (bf16[8,96,1024]{2,1,0:T(8,128)(2,1)}, bf16[8,96,1024]{2,1,0:T(8,128)(2,1)S(1)}, u32[]{:S(2)}) copy-start(bf16[8,96,1024]{2,1,0:T(8,128)(2,1)S(1)} %convolution_convert_fusion.2) | copy-start | bytes 4718596
  65.2 60.5 %copy-start.5 = (bf16[8,96,1024]{2,1,0:T(8,128)(2,1)}, bf16[8,96,1024]{2,1,0:T(8,128)(2,1)S(1)}, u32[]{:S(2)}) copy-start(bf16[8,96,1024]{2,1,0:T(8,128)(2,1)S(1)} %convolution_convert_fusion.3) | copy-start | bytes 4718596
  71.6 120.9 %reduce-scatter.12.cloned.1.call-start = ((), (), s32[]{:S(2)}) async-start(), calls=%async_computation.10 | async-start | bytes 3932160 | tf_op jit(solution)/shard_map/reduce_scatter | solution.py:53
  112.1 2.3 copy-start
  112.1 3.7 copy-start.14
  114.4 3.2 copy-start.11
  115.0 2.7 copy-start.9
  121.5 111.9 %reduce-scatter.6.cloned.1.call-start = ((), (), s32[]{:S(2)}) async-start(), calls=%async_computation.6 | async-start | bytes 3932160 | tf_op jit(solution)/shard_map/reduce_scatter | solution.py:53
  122.0 3.7 copy-start.18
  129.5 143.5 %all-gather.10.cloned.1.call-start = ((), (), s32[]{:S(2)}) async-start(), calls=%async_computation.8 | async-start | bytes 3932160 | tf_op jit(solution)/shard_map/all_gather | solution.py:58
  151.6 90.1 %copy-start.2 = (bf16[384,1024]{1,0:T(8,128)(2,1)S(1)}, bf16[384,1024]{1,0:T(8,128)(2,1)}, u32[]{:S(2)}) copy-start(bf16[384,1024]{1,0:T(8,128)(2,1)} %reduce-scatter.8.cloned.1.call-done) | copy-start | bytes 2359300
  192.5 49.2 %copy-start.3 = (bf16[384,1024]{1,0:T(8,128)(2,1)S(1)}, bf16[384,1024]{1,0:T(8,128)(2,1)}, u32[]{:S(2)}) copy-start(bf16[384,1024]{1,0:T(8,128)(2,1)} %reduce-scatter.12.cloned.1.call-done) | copy-start | bytes 2359300
  233.4 8.3 %copy-start.4 = (bf16[384,1024]{1,0:T(8,128)(2,1)S(1)}, bf16[384,1024]{1,0:T(8,128)(2,1)}, u32[]{:S(2)}) copy-start(bf16[384,1024]{1,0:T(8,128)(2,1)} %reduce-scatter.6.cloned.1.call-done) | copy-start | bytes 2359300
  244.3 59.3 %all-gather.14.cloned.1.call-start = ((), (), s32[]{:S(2)}) async-start(), calls=%async_computation.12 | async-start | bytes 3932160 | tf_op jit(solution)/shard_map/all_gather | solution.py:58
  245.1 89.2 %all-gather.12.cloned.1.call-start = ((), (), s32[]{:S(2)}) async-start(), calls=%async_computation.11 | async-start | bytes 3932160 | tf_op jit(solution)/shard_map/all_gather | solution.py:58
  245.8 161.0 %reduce-scatter.10.cloned.1.call-start = ((), (), s32[]{:S(2)}) async-start(), calls=%async_computation.9 | async-start | bytes 2359296 | tf_op jit(solution)/shard_map/reduce_scatter | solution.py:68
  273.0 4.8 copy-start.20
  283.1 195.1 %reduce-scatter.14.cloned.1.call-start = ((), (), s32[]{:S(2)}) async-start(), calls=%async_computation.13 | async-start | bytes 2359296 | tf_op jit(solution)/shard_map/reduce_scatter | solution.py:68
  334.3 4.9 copy-start.22
  340.6 3.2 copy-start.24
  347.8 12.2 %copy-start.13 = (s32[128,8]{0,1:T(8,128)S(1)}, s32[128,8]{0,1:T(8,128)}, u32[]{:S(2)}) copy-start(s32[128,8]{0,1:T(8,128)} %param.8) | copy-start | bytes 12292
  347.8 12.8 %copy-start.8 = (bf16[8,96,1024]{2,1,0:T(8,128)(2,1)S(1)}, bf16[8,96,1024]{2,1,0:T(8,128)(2,1)}, u32[]{:S(2)}) copy-start(bf16[8,96,1024]{2,1,0:T(8,128)(2,1)} %copy-done.7) | copy-start | bytes 4718596
  360.7 3.4 copy-start.6
  360.7 3.4 copy-start.25
  366.0 3.4 copy-start.23
  373.1 2.5 copy-start.12
  373.1 3.9 copy-start.21
  (4 other events, 8.4 us)
Sparse Core Ops, SparseCore 0:
  10.1 52.1 all-gather.15
  64.4 47.6 all-gather.17
  115.2 36.4 reduce-scatter.7
  154.6 37.8 reduce-scatter.11
  195.5 37.8 reduce-scatter.5
  244.5 28.4 all-gather.9
  275.1 28.4 all-gather.13
  305.8 28.4 all-gather.11
  338.4 68.3 reduce-scatter.9
  410.8 67.3 reduce-scatter.13
where the time goes:
time: 492 us; the launch traced here: 485 us
  waiting for transfers between devices  336 us (68%)
  matrix products  54.6 us (11%)
  blocking collectives  49.9 us (10%)
  other arithmetic  20.2 us (4%)
  between operations  14.8 us (3%)
  local copies, waits for them, and re-layouts  8.33 us (2%)
    reduce_scatter x3, waiting for transfers between devices, scatter_rows(): lax.psum_scatter(jnp.concatenate(parts, axis=0), 'tensor', scatter_dimens...  104 us
    reduce_scatter x2, waiting for transfers between devices, combine(): lax.psum_scatter(total_sum.astype(BF16), 'expert', scatter_dimension=0, t...  95.1 us
    all_gather x3, waiting for transfers between devices, gather_rows(): full = lax.all_gather(value.astype(BF16), 'tensor', axis=0, tiled=True)  74.2 us
    dot_general x27, matrix products, dot(): return jnp.einsum(form, left, right, preferred_element_type=F32)  54.6 us
    all_gather x1, waiting for transfers between devices, per_device(): cotangent_all = lax.all_gather(out_cotangent, 'expert', axis=0)  40.4 us
    all_gather x1, blocking collectives, per_device(): weights_all = lax.all_gather(dense_weight, 'expert', axis=0)  32.6 us
    all_gather x1, waiting for transfers between devices, per_device(): tokens_all = lax.all_gather(tokens, 'expert', axis=0)  20 us
    all_to_all x1, blocking collectives, per_device(): lax.all_to_all(pair_tok.transpose(1, 0, 2), 'expert', split_axis=0, conca...  12.2 us
  transfers between devices with their start and end apart: 10, of which 10 were waited for; matrix products, arithmetic and copies ran while one was open for 14% of the time, Pallas kernels for 0%

commit v1 on v0

--- a/solution.py
+++ b/solution.py
@@ -55,7 +55,16 @@
         ).astype(F32)
 
     def gather_rows(value):
-        full = lax.all_gather(value.astype(BF16), "tensor", axis=0, tiled=True)
+        array = value.astype(BF16)
+        ways, here = (lax.axis_size("tensor"), lax.axis_index("tensor"))
+        grown, reach = (array, 1)
+        while reach < ways:
+            theirs = lax.ppermute(grown, "tensor", [(d, d ^ reach) for d in range(ways)])
+            mine_first = jnp.concatenate([grown, theirs], axis=0)
+            theirs_first = jnp.concatenate([theirs, grown], axis=0)
+            grown = jnp.where(here & reach == 0, mine_first, theirs_first)
+            reach = 2 * reach
+        full = grown
         return full.reshape(local, slots, hidden)
 
     def combine(parts):

time: 492 us -> 450 us (0.915)
  waiting for transfers between devices: 336 us -> 282 us
  other arithmetic: 20.2 us -> 37.5 us
  matrix products: 54.6 us -> 48 us
    ppermute x0 -> x6, waiting for transfers between devices: none -> 83.7 us  [gather_rows(): lax.ppermute(grown, 'tensor', [(d, d ^ reach) for d in range(ways)])]
    all_gather x3 -> x0, waiting for transfers between devices: 74.2 us -> none  [gather_rows(): full = lax.all_gather(value.astype(BF16), 'tensor', axis=0, tiled=True)]
    reduce_scatter x2, waiting for transfers between devices: 95.1 us -> 32.7 us  [combine(): lax.psum_scatter(total_sum.astype(BF16), 'expert', scatter_dimension=0, t...]
    select_n x0 -> x6, other arithmetic: none -> 17.5 us  [gather_rows(): grown = jnp.where(here & reach == 0, mine_first, theirs_first)]
    dot_general x27, matrix products: 54.6 us -> 48 us  [dot(): return jnp.einsum(form, left, right, preferred_element_type=F32)]
  transfers between devices with their start and end apart: 10 -> 13, of which waited for: 10 -> 11; matrix products, arithmetic and copies ran while one was open for 14% -> 18% of each run, Pallas kernels for 0% -> 0%
where the time goes in v1:
time: 450 us; the launch traced here: 442 us
  waiting for transfers between devices  282 us (63%)
  blocking collectives  50 us (11%)
  matrix products  48 us (11%)
  other arithmetic  37.5 us (8%)
  between operations  14.8 us (3%)
  local copies, waits for them, and re-layouts  5.67 us (1%)
    reduce_scatter x3, waiting for transfers between devices, scatter_rows(): lax.psum_scatter(jnp.concatenate(parts, axis=0), 'tensor', scatter_dimens...  104 us
    ppermute x6, waiting for transfers between devices, gather_rows(): lax.ppermute(grown, 'tensor', [(d, d ^ reach) for d in range(ways)])  83.7 us
    dot_general x27, matrix products, dot(): return jnp.einsum(form, left, right, preferred_element_type=F32)  48 us
    all_gather x1, waiting for transfers between devices, per_device(): cotangent_all = lax.all_gather(out_cotangent, 'expert', axis=0)  40.4 us
    reduce_scatter x2, waiting for transfers between devices, combine(): lax.psum_scatter(total_sum.astype(BF16), 'expert', scatter_dimension=0, t...  32.7 us
    all_gather x1, blocking collectives, per_device(): weights_all = lax.all_gather(dense_weight, 'expert', axis=0)  32.6 us
    all_gather x1, waiting for transfers between devices, per_device(): tokens_all = lax.all_gather(tokens, 'expert', axis=0)  20 us
    select_n x6, other arithmetic, gather_rows(): grown = jnp.where(here & reach == 0, mine_first, theirs_first)  17.5 us
  transfers between devices with their start and end apart: 13, of which 11 were waited for; matrix products, arithmetic and copies ran while one was open for 18% of the time, Pallas kernels for 0%

profile of v1, /device:TPU:0, one launch (start us, length us, event | category | flops | bytes accessed | tf_op | source)
XLA Modules:
  0.0 442.4 jit_solution(11744010813135485296)
XLA Ops:
  9.4 32.6 %all-gather = f32[1024,16]{0,1:T(8,128)S(1)} all-gather(f32[128,16]{0,1:T(8,128)S(1)} %select_reduce_fusion.3), channel_id=2, replica_groups=mesh['expert'=8,'tensor'=4] {'expert'}, dimensions={0}, use_global_device_ids=true | all-gather | bytes 73728 | tf_op jit(solution)/shard_map/all_gather | solution.py:31
  42.3 20.0 %all-gather.7.cloned.1.call-done = bf16[1024,1024]{1,0:T(8,128)(2,1)} async-done(((bf16[128,1024]{1,0:T(8,128)(2,1)}), bf16[1024,1024]{1,0:T(8,128)(2,1)}) %all-gather.7.cloned.1.call-update) | async-done | bytes 2097168 | tf_op jit(solution)/shard_map/all_gather | solution.py:32
  62.3 2.3 convolution_convert_fusion.2
  69.7 2.0 pad_maximum_fusion.4
  71.7 40.4 %all-gather.9.cloned.1.call-done = bf16[1024,1024]{1,0:T(8,128)(2,1)} async-done(((bf16[128,1024]{1,0:T(8,128)(2,1)}), bf16[1024,1024]{1,0:T(8,128)(2,1)}) %all-gather.9.cloned.1.call-update) | async-done | bytes 2097168 | tf_op jit(solution)/shard_map/all_gather | solution.py:33
  112.1 2.3 convolution_convert_fusion
  119.5 2.0 pad_maximum_fusion.5
  122.1 3.6 fusion.40
  127.5 2.0 pad_maximum_fusion.3
  129.6 22.1 %reduce-scatter.8.cloned.1.call-done = bf16[384,1024]{1,0:T(8,128)(2,1)} async-done(((bf16[1536,1024]{1,0:T(8,128)(2,1)}), bf16[384,1024]{1,0:T(8,128)(2,1)}) %reduce-scatter.8.cloned.1.call-update) | async-done | bytes 786448 | tf_op jit(solution)/shard_map/reduce_scatter | solution.py:53
  151.7 40.9 %reduce-scatter.12.cloned.1.call-done = bf16[384,1024]{1,0:T(8,128)(2,1)} async-done(((bf16[1536,1024]{1,0:T(8,128)(2,1)}), bf16[384,1024]{1,0:T(8,128)(2,1)}) %reduce-scatter.12.cloned.1.call-update) | async-done | bytes 786448 | tf_op jit(solution)/shard_map/reduce_scatter | solution.py:53
  192.5 40.9 %reduce-scatter.6.cloned.1.call-done = bf16[384,1024]{1,0:T(8,128)(2,1)} async-done(((bf16[1536,1024]{1,0:T(8,128)(2,1)}), bf16[384,1024]{1,0:T(8,128)(2,1)}) %reduce-scatter.6.cloned.1.call-update) | async-done | bytes 786448 | tf_op jit(solution)/shard_map/reduce_scatter | solution.py:53
  233.4 2.3 fusion.65
  235.7 5.2 %all-gather.3 = f32[4,1,384]{2,1,0:T(1,128)S(1)} all-gather(f32[1,1,384]{2,1,0:T(1,128)S(1)} %reshape.84), channel_id=1, replica_groups=mesh['expert'=8,'tensor'=4] {'tensor'}, dimensions={0}, use_global_device_ids=true | all-gather | bytes 7680 | tf_op jit(solution)/shard_map/all_gather | solution.py:100
  241.8 2.3 fusion.64
  246.4 2.1 maximum_select_fusion.3
  251.3 2.7 maximum_select_fusion.5
  255.7 3.8 maximum_select_fusion.4
  259.9 26.0 %collective-permute-done.1 = bf16[768,1024]{1,0:T(8,128)(2,1)} collective-permute-done((bf16[768,1024]{1,0:T(8,128)(2,1)S(1)}, bf16[768,1024]{1,0:T(8,128)(2,1)}, u32[]{:S(2)}, u32[]{:S(2)}) %collective-permute-start.1) | collective-permute-done | bytes 1572896 | tf_op jit(solution)/shard_map/ppermute | solution.py:62
  285.9 2.8 maximum_select_fusion
  293.1 2.1 add_convert_fusion.1
  295.5 24.1 %collective-permute-done.5 = bf16[768,1024]{1,0:T(8,128)(2,1)} collective-permute-done((bf16[768,1024]{1,0:T(8,128)(2,1)S(1)}, bf16[768,1024]{1,0:T(8,128)(2,1)}, u32[]{:S(2)}, u32[]{:S(2)}) %collective-permute-start.5) | collective-permute-done | bytes 1572896 | tf_op jit(solution)/shard_map/ppermute | solution.py:62
  319.6 2.8 maximum_select_fusion.2
  322.4 30.3 %collective-permute-done.3 = bf16[768,1024]{1,0:T(8,128)(2,1)} collective-permute-done((bf16[768,1024]{1,0:T(8,128)(2,1)}, bf16[768,1024]{1,0:T(8,128)(2,1)}, u32[]{:S(2)}, u32[]{:S(2)}) %collective-permute-start.3) | collective-permute-done | bytes 1572896 | tf_op jit(solution)/shard_map/ppermute | solution.py:62
  352.7 3.3 maximum_select_fusion.1
  364.5 2.2 add_convert_fusion
  366.8 12.2 %all_to_all.5 = f32[8,2,128]{2,1,0:T(2,128)S(1)} all-to-all(f32[8,2,128]{2,1,0:T(2,128)S(1)} %copy.26), channel_id=1, replica_groups=mesh['expert'=8,'tensor'=4] {'expert'}, dimensions={0} | all-to-all | bytes 16384 | tf_op jit(solution)/shard_map/all_to_all | solution.py:103
  379.6 3.4 convert_bitcast_fusion.4
  384.9 2.5 pad_maximum_fusion
  392.6 2.5 pad_maximum_fusion.1
  400.2 2.4 pad_maximum_fusion.2
  402.6 32.7 %reduce-scatter.14.cloned.1.call-done = bf16[1,128,1024]{2,1,0:T(8,128)(2,1)} async-done(((bf16[8,128,1024]{2,1,0:T(8,128)(2,1)}), bf16[1,128,1024]{2,1,0:T(8,128)(2,1)}) %reduce-scatter.14.cloned.1.call-update) | async-done | bytes 262160 | tf_op jit(solution)/shard_map/reduce_scatter | solution.py:77
  (109 shorter events, 48.8 us)
Async XLA Ops:
  7.2 55.1 %all-gather.7.cloned.1.call-start = ((), (), s32[]{:S(2)}) async-start(), calls=%async_computation.11 | async-start | bytes 2359296 | tf_op jit(solution)/shard_map/all_gather | solution.py:32
  7.9 104.2 %all-gather.9.cloned.1.call-start = ((), (), s32[]{:S(2)}) async-start(), calls=%async_computation.12 | async-start | bytes 2359296 | tf_op jit(solution)/shard_map/all_gather | solution.py:33
  8.6 143.0 %reduce-scatter.8.cloned.1.call-start = ((), (), s32[]{:S(2)}) async-start(), calls=%async_computation.7 | async-start | bytes 3932160 | tf_op jit(solution)/shard_map/reduce_scatter | solution.py:53
  62.3 3.8 copy-start.22
  64.6 57.4 %copy-start.13 = (bf16[8,96,1024]{2,1,0:T(8,128)(2,1)}, bf16[8,96,1024]{2,1,0:T(8,128)(2,1)S(1)}, u32[]{:S(2)}) copy-start(bf16[8,96,1024]{2,1,0:T(8,128)(2,1)S(1)} %convolution_convert_fusion.2) | copy-start | bytes 4718596
  65.2 60.5 %copy-start.11 = (bf16[8,96,1024]{2,1,0:T(8,128)(2,1)}, bf16[8,96,1024]{2,1,0:T(8,128)(2,1)S(1)}, u32[]{:S(2)}) copy-start(bf16[8,96,1024]{2,1,0:T(8,128)(2,1)S(1)} %convolution_convert_fusion.3) | copy-start | bytes 4718596
  71.6 120.9 %reduce-scatter.12.cloned.1.call-start = ((), (), s32[]{:S(2)}) async-start(), calls=%async_computation.9 | async-start | bytes 3932160 | tf_op jit(solution)/shard_map/reduce_scatter | solution.py:53
  112.1 3.8 copy-start.20
  114.4 3.3 copy-start.17
  121.5 111.9 %reduce-scatter.6.cloned.1.call-start = ((), (), s32[]{:S(2)}) async-start(), calls=%async_computation.6 | async-start | bytes 3932160 | tf_op jit(solution)/shard_map/reduce_scatter | solution.py:53
  122.0 3.7 copy-start.24
  129.5 273.0 %reduce-scatter.10.cloned.1.call-start = ((), (), s32[]{:S(2)}) async-start(), calls=%async_computation.8 | async-start | bytes 2359296 | tf_op jit(solution)/shard_map/reduce_scatter | solution.py:77
  151.7 90.1 %copy-start.6 = (bf16[384,1024]{1,0:T(8,128)(2,1)S(1)}, bf16[384,1024]{1,0:T(8,128)(2,1)}, u32[]{:S(2)}) copy-start(bf16[384,1024]{1,0:T(8,128)(2,1)} %reduce-scatter.8.cloned.1.call-done) | copy-start | bytes 2359300
  192.5 49.2 %copy-start.7 = (bf16[384,1024]{1,0:T(8,128)(2,1)S(1)}, bf16[384,1024]{1,0:T(8,128)(2,1)}, u32[]{:S(2)}) copy-start(bf16[384,1024]{1,0:T(8,128)(2,1)} %reduce-scatter.12.cloned.1.call-done) | copy-start | bytes 2359300
  233.4 8.3 %copy-start.8 = (bf16[384,1024]{1,0:T(8,128)(2,1)S(1)}, bf16[384,1024]{1,0:T(8,128)(2,1)}, u32[]{:S(2)}) copy-start(bf16[384,1024]{1,0:T(8,128)(2,1)} %reduce-scatter.6.cloned.1.call-done) | copy-start | bytes 2359300
  244.1 4.8 %copy-start.9 = (bf16[384,1024]{1,0:T(8,128)(2,1)S(1)}, bf16[384,1024]{1,0:T(8,128)(2,1)}, u32[]{:S(2)}) copy-start(bf16[384,1024]{1,0:T(8,128)(2,1)} %get-tuple-element.9) | copy-start | bytes 2359300
  244.1 2.3 collective-permute-start
  248.5 37.4 %collective-permute-start.1 = (bf16[768,1024]{1,0:T(8,128)(2,1)S(1)}, bf16[768,1024]{1,0:T(8,128)(2,1)}, u32[]{:S(2)}, u32[]{:S(2)}) collective-permute-start(bf16[768,1024]{1,0:T(8,128)(2,1)S(1)} %maximum_select_fusion.3), channel_id=1, source_target_pairs={{0,2},{1,3},{2,0},{3,1},{4,6},{5,7},{6,4},{7,5},{8,10},{9,11},{10,... | collective-permute-start | bytes 4718600 | tf_op jit(solution)/shard_map/ppermute | solution.py:62
  248.9 2.4 collective-permute-start.4
  249.0 6.8 %collective-permute-start.2 = (bf16[384,1024]{1,0:T(8,128)(2,1)}, bf16[384,1024]{1,0:T(8,128)(2,1)}, u32[]{:S(2)}, u32[]{:S(2)}) collective-permute-start(bf16[384,1024]{1,0:T(8,128)(2,1)} %get-tuple-element.8), channel_id=1, source_target_pairs={{0,1},{1,0},{2,3},{3,2},{4,5},{5,4},{6,7},{7,6},{8,9},{9,8},{10,11... | collective-permute-start | bytes 2359304 | tf_op jit(solution)/shard_map/ppermute | solution.py:62
  254.0 65.7 %collective-permute-start.5 = (bf16[768,1024]{1,0:T(8,128)(2,1)S(1)}, bf16[768,1024]{1,0:T(8,128)(2,1)}, u32[]{:S(2)}, u32[]{:S(2)}) collective-permute-start(bf16[768,1024]{1,0:T(8,128)(2,1)S(1)} %maximum_select_fusion.5), channel_id=1, source_target_pairs={{0,2},{1,3},{2,0},{3,1},{4,6},{5,7},{6,4},{7,5},{8,10},{9,11},{10,... | collective-permute-start | bytes 4718600 | tf_op jit(solution)/shard_map/ppermute | solution.py:62
  259.6 29.1 %copy-start.21 = (bf16[2,1024,1024]{2,1,0:T(8,128)(2,1)S(1)}, bf16[2,1024,1024]{2,1,0:T(8,128)(2,1)}, u32[]{:S(2)}) copy-start(bf16[2,1024,1024]{2,1,0:T(8,128)(2,1)} %param.12) | copy-start | bytes 12582916
  259.6 93.1 %collective-permute-start.3 = (bf16[768,1024]{1,0:T(8,128)(2,1)}, bf16[768,1024]{1,0:T(8,128)(2,1)}, u32[]{:S(2)}, u32[]{:S(2)}) collective-permute-start(bf16[768,1024]{1,0:T(8,128)(2,1)} %maximum_select_fusion.4), channel_id=1, source_target_pairs={{0,2},{1,3},{2,0},{3,1},{4,6},{5,7},{6,4},{7,5},{8,10},{9,11},{10,... | collective-permute-start | bytes 4718600 | tf_op jit(solution)/shard_map/ppermute | solution.py:62
  295.3 140.0 %reduce-scatter.14.cloned.1.call-start = ((), (), s32[]{:S(2)}) async-start(), calls=%async_computation.10 | async-start | bytes 2359296 | tf_op jit(solution)/shard_map/reduce_scatter | solution.py:77
  322.4 38.5 %copy-start.4 = (bf16[1536,1024]{1,0:T(8,128)(2,1)}, bf16[1536,1024]{1,0:T(8,128)(2,1)S(1)}, u32[]{:S(2)}) copy-start(bf16[1536,1024]{1,0:T(8,128)(2,1)S(1)} %maximum_select_fusion.2) | copy-start | bytes 9437188
  322.4 33.6 %copy-start.23 = (bf16[2,1024,1024]{2,1,0:T(8,128)(2,1)S(1)}, bf16[2,1024,1024]{2,1,0:T(8,128)(2,1)}, u32[]{:S(2)}) copy-start(bf16[2,1024,1024]{2,1,0:T(8,128)(2,1)} %param.11) | copy-start | bytes 12582916
  366.7 12.3 %copy-start.19 = (s32[128,8]{0,1:T(8,128)S(1)}, s32[128,8]{0,1:T(8,128)}, u32[]{:S(2)}) copy-start(s32[128,8]{0,1:T(8,128)} %param.8) | copy-start | bytes 12292
  379.6 3.4 copy-start.12
  384.9 3.3 copy-start.5
  384.9 3.9 copy-start.14
  392.5 3.3 copy-start.3
  392.6 3.9 copy-start.18
  (7 other events, 14.1 us)
Sparse Core Ops, SparseCore 0:
  10.1 52.1 all-gather.6
  64.4 47.6 all-gather.8
  115.2 36.4 reduce-scatter.7
  154.6 37.8 reduce-scatter.11
  195.5 37.8 reduce-scatter.5
  295.4 68.2 reduce-scatter.9
  367.8 67.4 reduce-scatter.13
